TPU v7x, 32 devices: a whole 2x2x4 slice. The times are simulated.
32 devices in a mesh: gx: 2 (over x), gy: 4 (over y, core), gz: 4 (over z).
Axes of the slice: x: 2, y: 2, z: 4, core: 2. Of those that a mesh axis runs over, the one named last changes fastest.
Arguments:
- residual: bfloat16 [2, 4, 4, 3, 256, 256], P('gx', 'gy', 'gz'), may hold values from -6 to 6
- face_basis: bfloat16 [2, 4, 4, 3, 256, 256], P('gx', 'gy', 'gz'), may hold values from -0.375 to 0.375
- factor: bfloat16 [2, 4, 4, 768, 768], P('gx', 'gy', 'gz'), may hold values from -0.21875 to 0.21875
- coarse_inv: bfloat16 [2, 4, 4, 768, 768], P('gx', 'gy', 'gz'), may hold values from -0.21875 to 0.21875
- item_owner: int32 [2, 4, 4, 24], P('gx', 'gy', 'gz'), may hold values from 0 to 3, as said below
Outputs:
- result: bfloat16 [2, 4, 4, 3, 256, 256], P('gx', 'gy', 'gz')
Inputs may be any that keep to these rules, and one draw needn't show every extreme that they name: `item_owner`: within the groups of one subdomain, at most 12 name the same owner, and in every subdomain some owner is named exactly 12 times.
All inputs are finite; a program needn't handle non-finite values.
Results may differ from a plain program's by a relative error of at most 0.006.
Values may be sent and summed in bfloat16 or wider, within the bound.
No kernel may reach another device: no remote copies, remote signals or barrier semaphores. Data moves between devices by JAX's collectives and lax.ppermute only.
A program may use at most 64 MiB of HBM per device.

v0:
```python
import jax
import jax.numpy as jnp
from jax import lax
from jax.sharding import PartitionSpec as P

PF = 128
GROUP = 16
ITEMS = 24


def shifted(block, axis, distance):
    devices = range(lax.axis_size(axis))
    route = [((i - distance) % len(devices), i) for i in devices]
    return lax.ppermute(block, axis, route)


def along_axes(faces, offset):
    from_x = shifted(faces[0], "gx", offset)
    from_y = shifted(faces[1], "gy", offset)
    from_z = shifted(faces[2], "gz", offset)
    return jnp.stack([from_x, from_y, from_z])


def apply_coarse(matrix, block):
    rows = block.shape[3]
    stacked = block.reshape(-1, rows)
    answer = lax.dot_general(
        matrix, stacked, (((0,), (0,)), ((), ())), preferred_element_type=jnp.float32
    )
    return answer.astype(jnp.bfloat16).reshape(block.shape)


def rank_within(owners):
    item_index = jnp.arange(owners.shape[-1], dtype=jnp.int32)
    same_owner = owners[..., :, None] == owners[..., None, :]
    earlier = item_index[:, None] > item_index[None, :]
    return jnp.sum((same_owner & earlier).astype(jnp.int32), axis=-1)


def body(residual, face_basis, factor, coarse_inv, item_owner):
    local_resid = residual[0, 0, 0]
    local_basis = face_basis[0, 0, 0]
    local_factor = factor[0, 0, 0]
    local_coarse = coarse_inv[0, 0, 0]
    owners = item_owner[0, 0, 0]
    columns = local_resid.shape[-1]
    column_size = lax.axis_size("gz")
    send_cap = local_coarse.shape[0] // (column_size * GROUP)
    transformed = jnp.einsum(
        "fac,far->fcr", local_basis, local_resid, preferred_element_type=jnp.float32
    )
    primal_items = transformed[:, :PF, :].astype(jnp.bfloat16).reshape(ITEMS, GROUP, columns)
    dual_own = transformed[:, PF:, :].astype(jnp.bfloat16)
    slot_rank = rank_within(owners)
    send_slot = owners * send_cap + slot_rank
    dual_in = along_axes(dual_own, 1)
    dual_load = (jnp.concatenate([dual_in, dual_own], axis=0) * 0.5).reshape(-1, columns)
    half_solve = lax.dot_general(
        local_factor, dual_load, (((0,), (0,)), ((), ())), preferred_element_type=jnp.float32
    ).astype(jnp.bfloat16)
    solved = (
        jnp.dot(local_factor, half_solve, preferred_element_type=jnp.float32)
        .astype(jnp.bfloat16)
        .reshape(6, -1, columns)
    )
    from_above = along_axes(solved[:3], -1)
    dual_part = (0.5 * (solved[3:].astype(jnp.float32) + from_above.astype(jnp.float32))).astype(
        jnp.bfloat16
    )
    outgoing = jnp.zeros((column_size * send_cap, GROUP, columns), jnp.bfloat16)
    outgoing = (
        outgoing.at[send_slot].set(primal_items).reshape(column_size, send_cap, GROUP, columns)
    )
    answer = apply_coarse(
        local_coarse, lax.all_to_all(outgoing, "gz", split_axis=0, concat_axis=0, tiled=True)
    )
    returned = lax.all_to_all(answer, "gz", split_axis=0, concat_axis=0, tiled=True)
    flat_back = returned.reshape(column_size * send_cap, GROUP, columns)
    primal_part = jnp.take(flat_back, send_slot, axis=0).reshape(3, PF, columns)
    combined = jnp.concatenate([primal_part, dual_part], axis=1)
    result = jnp.einsum("fac,fcr->far", local_basis, combined, preferred_element_type=jnp.float32)
    return result.astype(jnp.bfloat16)[None, None, None]


def solution(mesh):
    in_specs = (
        P("gx", "gy", "gz", None, None, None),
        P("gx", "gy", "gz", None, None, None),
        P("gx", "gy", "gz", None, None),
        P("gx", "gy", "gz", None, None),
        P("gx", "gy", "gz", None),
    )
    out_specs = P("gx", "gy", "gz", None, None, None)
    return jax.shard_map(body, mesh=mesh, in_specs=in_specs, out_specs=out_specs, check_vma=False)
```

profile of v0, /device:TPU:0, one launch (start us, length us, event | category | flops | bytes accessed | tf_op | source)
XLA Modules:
  0.0 49.0 jit_solution(11675209019695398291)
XLA Ops:
  0.0 0.0 copy-start
  0.0 0.0 copy-start.2
  0.0 1.5 %convolution_convert_fusion.4 = bf16[3,256,256]{2,1,0:T(8,128)(2,1)S(1)} fusion(bf16[1,1,1,3,256,256]{5,4,3,2,1,0:T(8,128)(2,1)} %param.5, bf16[1,1,1,3,256,256]{5,4,3,2,1,0:T(8,128)(2,1)} %param.6), kind=kOutput, calls=%fused_computation.6 | convolution fusion | flops 100859904 | bytes 1179648 | tf_op jit(solution)/shard_map/fac,far->fcr/dot_general | solution.py:49
  1.6 3.0 %collective-permute-start = (bf16[128,256]{1,0:T(8,128)(2,1)S(1)}, bf16[128,256]{1,0:T(8,128)(2,1)S(1)}, u32[]{:S(2)}, u32[]{:S(2)}) collective-permute-start(bf16[128,256]{1,0:T(8,128)(2,1)S(1)} %get-tuple-element.10), channel_id=1, source_target_pairs={{16,0},{0,16},{17,1},{1,17},{18,2},{2,18},{19,3},{3,19},{20,4},{4,... | collective-permute-start | bytes 196616 | tf_op jit(solution)/shard_map/ppermute | solution.py:14
  4.6 0.0 collective-permute-start.1
  4.6 1.6 %collective-permute-start.2 = (bf16[128,256]{1,0:T(8,128)(2,1)S(1)}, bf16[128,256]{1,0:T(8,128)(2,1)S(1)}, u32[]{:S(2)}, u32[]{:S(2)}) collective-permute-start(bf16[128,256]{1,0:T(8,128)(2,1)S(1)} %get-tuple-element.11), channel_id=1, source_target_pairs={{3,0},{0,1},{1,2},{2,3},{7,4},{4,5},{5,6},{6,7},{11,8},{8,9},{9,10... | collective-permute-start | bytes 196616 | tf_op jit(solution)/shard_map/ppermute | solution.py:14
  6.2 0.0 copy-done.2
  6.2 0.2 convert_reduce_fusion
  6.4 0.8 %broadcast_in_dim.26 = bf16[48,16,256]{2,1,0:T(8,128)(2,1)} broadcast(bf16[]{:T(256)} %constant.12.clone.1), dimensions={} | broadcast | bytes 393218 | tf_op jit(solution)/shard_map/broadcast_in_dim | solution.py:70
  7.2 3.9 %scatter_fusion = bf16[48,16,256]{2,1,0:T(8,128)(2,1)} fusion(bf16[48,16,256]{2,1,0:T(8,128)(2,1)} %broadcast_in_dim.26, s32[24]{0:T(128)S(1)} %fusion.13, bf16[24,16,256]{2,1,0:T(8,128)(2,1)S(1)} %bitcast.57), kind=kCustom, calls=%fused_computation.1 | custom fusion | bytes 589920 | tf_op jit(solution)/shard_map/scatter | solution.py:72
  11.1 3.9 %all-to-all-start = ((bf16[4,12,16,256]{3,2,1,0:T(8,128)(2,1)}), bf16[4,12,16,256]{3,2,1,0:T(8,128)(2,1)S(1)}, u32[]{:S(2)}, u32[]{:S(2)}) async-start(bf16[4,12,16,256]{3,2,1,0:T(8,128)(2,1)} %bitcast.7), calls=%async_computation | async-start | bytes 786432 | tf_op jit(solution)/shard_map/all_to_all | solution.py:75
  14.9 0.1 reduce_sum.14
  15.0 0.1 mul.42
  15.1 0.1 broadcast_in_dim.23
  15.2 0.1 broadcast_in_dim.24
  15.3 0.0 collective-permute-done
  15.3 0.0 collective-permute-done.1
  15.3 0.0 collective-permute-done.2
  15.3 0.1 maximum_multiply_fusion
  15.4 0.0 copy-done
  15.4 1.0 %fusion.2 = bf16[768,256]{0,1:T(8,128)(2,1)S(1)} fusion(bf16[768,256]{1,0:T(8,128)(2,1)S(1)} %bitcast.59, bf16[1,1,1,768,768]{4,3,2,1,0:T(8,128)(2,1)S(1)} %copy-done), kind=kOutput, calls=%fused_computation.9 | convolution fusion | flops 604372992 | bytes 1966080 | tf_op jit(solution)/shard_map/dot_general | solution.py:62
  16.4 11.5 %all-to-all-done = bf16[4,12,16,256]{3,2,1,0:T(8,128)(2,1)S(1)} async-done(((bf16[4,12,16,256]{3,2,1,0:T(8,128)(2,1)}), bf16[4,12,16,256]{3,2,1,0:T(8,128)(2,1)S(1)}, u32[]{:S(2)}, u32[]{:S(2)}) %all-to-all-start) | async-done | bytes 393248 | tf_op jit(solution)/shard_map/all_to_all | solution.py:75
  27.9 1.8 %fusion.1 = bf16[768,256]{0,1:T(8,128)(2,1)S(1)} fusion(bf16[768,256]{1,0:T(8,128)(2,1)S(1)} %bitcast.58, bf16[1,1,1,768,768]{4,3,2,1,0:T(8,128)(2,1)} %param.8), kind=kOutput, calls=%fused_computation.8 | convolution fusion | flops 302186496 | bytes 1966080 | tf_op jit(solution)/shard_map/dot_general | solution.py:27
  29.7 0.9 %copy.15 = bf16[768,256]{1,0:T(8,128)(2,1)} copy(bf16[768,256]{0,1:T(8,128)(2,1)S(1)} %fusion.1) | data formatting | bytes 786432 | tf_op jit(solution)/shard_map/convert_element_type | solution.py:30
  30.6 3.5 %all-to-all-start.1 = ((bf16[4,12,16,256]{3,2,1,0:T(8,128)(2,1)}), bf16[4,12,16,256]{3,2,1,0:T(8,128)(2,1)S(1)}, u32[]{:S(2)}, u32[]{:S(2)}) async-start(bf16[4,12,16,256]{3,2,1,0:T(8,128)(2,1)} %bitcast.11), calls=%async_computation.1 | async-start | bytes 786432 | tf_op jit(solution)/shard_map/all_to_all | solution.py:77
  34.1 0.6 %collective-permute-start.3 = (bf16[128,256]{0,1:T(8,128)(2,1)S(1)}, bf16[128,256]{0,1:T(8,128)(2,1)S(1)}, u32[]{:S(2)}, u32[]{:S(2)}) collective-permute-start(bf16[128,256]{0,1:T(8,128)(2,1)S(1)} %get-tuple-element.7), channel_id=1, source_target_pairs={{16,0},{0,16},{17,1},{1,17},{18,2},{2,18},{19,3},{3,19},{20,4},{4,... | collective-permute-start | bytes 196616 | tf_op jit(solution)/shard_map/ppermute | solution.py:14
  34.7 0.0 collective-permute-start.4
  34.7 3.8 %collective-permute-start.5 = (bf16[128,256]{0,1:T(8,128)(2,1)S(1)}, bf16[128,256]{0,1:T(8,128)(2,1)S(1)}, u32[]{:S(2)}, u32[]{:S(2)}) collective-permute-start(bf16[128,256]{0,1:T(8,128)(2,1)S(1)} %get-tuple-element.8), channel_id=1, source_target_pairs={{1,0},{2,1},{3,2},{0,3},{5,4},{6,5},{7,6},{4,7},{9,8},{10,9},{11,1... | collective-permute-start | bytes 196616 | tf_op jit(solution)/shard_map/ppermute | solution.py:14
  38.5 0.2 copy.17
  38.7 0.2 copy.18
  38.9 0.0 copy-start.1
  38.9 0.0 collective-permute-done.3
  38.9 0.0 collective-permute-done.4
  38.9 4.4 %collective-permute-done.5 = bf16[128,256]{0,1:T(8,128)(2,1)S(1)} collective-permute-done((bf16[128,256]{0,1:T(8,128)(2,1)S(1)}, bf16[128,256]{0,1:T(8,128)(2,1)S(1)}, u32[]{:S(2)}, u32[]{:S(2)}) %collective-permute-start.5) | collective-permute-done | bytes 65568 | tf_op jit(solution)/shard_map/ppermute | solution.py:14
  43.3 0.1 multiply_convert_fusion
  43.4 3.6 %all-to-all-done.1 = bf16[4,12,16,256]{3,2,1,0:T(8,128)(2,1)S(1)} async-done(((bf16[4,12,16,256]{3,2,1,0:T(8,128)(2,1)}), bf16[4,12,16,256]{3,2,1,0:T(8,128)(2,1)S(1)}, u32[]{:S(2)}, u32[]{:S(2)}) %all-to-all-start.1) | async-done | bytes 393248 | tf_op jit(solution)/shard_map/all_to_all | solution.py:77
  47.0 0.6 %gather_fusion = bf16[24,16,256]{2,1,0:T(8,128)(2,1)S(1)} fusion(bf16[48,16,256]{2,1,0:T(8,128)(2,1)S(1)} %bitcast.55, s32[1024]{0:T(1024)S(1)} %pad_clamp_fusion), kind=kCustom, calls=%fused_computation | custom fusion | bytes 393312 | tf_op jit(solution)/shard_map/jit(_take)/gather | solution.py:79
  47.6 0.2 copy.16
  47.7 0.0 copy-done.1
  47.8 0.3 fusion
  48.1 0.9 %copy.19 = bf16[1,1,1,3,256,256]{5,4,3,2,1,0:T(8,128)(2,1)} copy(bf16[1,1,1,3,256,256]{4,5,3,2,1,0:T(8,128)(2,1)S(1)} %fusion) | data formatting | bytes 786432 | tf_op jit(solution)/shard_map/broadcast_in_dim | solution.py:82
  (9 shorter events, 0.2 us)
Async XLA Ops:
  0.0 15.4 %copy-start = (bf16[1,1,1,768,768]{4,3,2,1,0:T(8,128)(2,1)S(1)}, bf16[1,1,1,768,768]{4,3,2,1,0:T(8,128)(2,1)}, u32[]{:S(2)}) copy-start(bf16[1,1,1,768,768]{4,3,2,1,0:T(8,128)(2,1)} %param.7) | copy-start | bytes 3538948
  0.0 6.2 %copy-start.2 = (s32[1,1,1,24]{3,2,1,0:T(1,128)S(1)}, s32[1,1,1,24]{3,2,1,0:T(1,128)}, u32[]{:S(2)}) copy-start(s32[1,1,1,24]{3,2,1,0:T(1,128)} %param.9) | copy-start | bytes 292
  1.6 13.7 %collective-permute-start = (bf16[128,256]{1,0:T(8,128)(2,1)S(1)}, bf16[128,256]{1,0:T(8,128)(2,1)S(1)}, u32[]{:S(2)}, u32[]{:S(2)}) collective-permute-start(bf16[128,256]{1,0:T(8,128)(2,1)S(1)} %get-tuple-element.10), channel_id=1, source_target_pairs={{16,0},{0,16},{17,1},{1,17},{18,2},{2,18},{19,3},{3,19},{20,4},{4,... | collective-permute-start | bytes 196616 | tf_op jit(solution)/shard_map/ppermute | solution.py:14
  4.6 10.7 %collective-permute-start.1 = (bf16[128,256]{1,0:T(8,128)(2,1)S(1)}, bf16[128,256]{1,0:T(8,128)(2,1)S(1)}, u32[]{:S(2)}, u32[]{:S(2)}) collective-permute-start(bf16[128,256]{1,0:T(8,128)(2,1)S(1)} %get-tuple-element.12), channel_id=1, source_target_pairs={{12,0},{0,4},{4,8},{8,12},{13,1},{1,5},{5,9},{9,13},{14,2},{2,6},{... | collective-permute-start | bytes 196616 | tf_op jit(solution)/shard_map/ppermute | solution.py:14
  4.6 10.7 %collective-permute-start.2 = (bf16[128,256]{1,0:T(8,128)(2,1)S(1)}, bf16[128,256]{1,0:T(8,128)(2,1)S(1)}, u32[]{:S(2)}, u32[]{:S(2)}) collective-permute-start(bf16[128,256]{1,0:T(8,128)(2,1)S(1)} %get-tuple-element.11), channel_id=1, source_target_pairs={{3,0},{0,1},{1,2},{2,3},{7,4},{4,5},{5,6},{6,7},{11,8},{8,9},{9,10... | collective-permute-start | bytes 196616 | tf_op jit(solution)/shard_map/ppermute | solution.py:14
  11.1 16.9 %all-to-all-start = ((bf16[4,12,16,256]{3,2,1,0:T(8,128)(2,1)}), bf16[4,12,16,256]{3,2,1,0:T(8,128)(2,1)S(1)}, u32[]{:S(2)}, u32[]{:S(2)}) async-start(bf16[4,12,16,256]{3,2,1,0:T(8,128)(2,1)} %bitcast.7), calls=%async_computation | async-start | bytes 786432 | tf_op jit(solution)/shard_map/all_to_all | solution.py:75
  30.6 16.4 %all-to-all-start.1 = ((bf16[4,12,16,256]{3,2,1,0:T(8,128)(2,1)}), bf16[4,12,16,256]{3,2,1,0:T(8,128)(2,1)S(1)}, u32[]{:S(2)}, u32[]{:S(2)}) async-start(bf16[4,12,16,256]{3,2,1,0:T(8,128)(2,1)} %bitcast.11), calls=%async_computation.1 | async-start | bytes 786432 | tf_op jit(solution)/shard_map/all_to_all | solution.py:77
  34.1 4.8 %collective-permute-start.3 = (bf16[128,256]{0,1:T(8,128)(2,1)S(1)}, bf16[128,256]{0,1:T(8,128)(2,1)S(1)}, u32[]{:S(2)}, u32[]{:S(2)}) collective-permute-start(bf16[128,256]{0,1:T(8,128)(2,1)S(1)} %get-tuple-element.7), channel_id=1, source_target_pairs={{16,0},{0,16},{17,1},{1,17},{18,2},{2,18},{19,3},{3,19},{20,4},{4,... | collective-permute-start | bytes 196616 | tf_op jit(solution)/shard_map/ppermute | solution.py:14
  34.7 4.2 %collective-permute-start.4 = (bf16[128,256]{0,1:T(8,128)(2,1)S(1)}, bf16[128,256]{0,1:T(8,128)(2,1)S(1)}, u32[]{:S(2)}, u32[]{:S(2)}) collective-permute-start(bf16[128,256]{0,1:T(8,128)(2,1)S(1)} %get-tuple-element.9), channel_id=1, source_target_pairs={{4,0},{8,4},{12,8},{0,12},{5,1},{9,5},{13,9},{1,13},{6,2},{10,6},{... | collective-permute-start | bytes 196616 | tf_op jit(solution)/shard_map/ppermute | solution.py:14
  34.7 8.6 %collective-permute-start.5 = (bf16[128,256]{0,1:T(8,128)(2,1)S(1)}, bf16[128,256]{0,1:T(8,128)(2,1)S(1)}, u32[]{:S(2)}, u32[]{:S(2)}) collective-permute-start(bf16[128,256]{0,1:T(8,128)(2,1)S(1)} %get-tuple-element.8), channel_id=1, source_target_pairs={{1,0},{2,1},{3,2},{0,3},{5,4},{6,5},{7,6},{4,7},{9,8},{10,9},{11,1... | collective-permute-start | bytes 196616 | tf_op jit(solution)/shard_map/ppermute | solution.py:14
  38.9 8.9 %copy-start.1 = (bf16[1,1,1,3,256,256]{5,4,3,2,1,0:T(8,128)(2,1)S(1)}, bf16[1,1,1,3,256,256]{5,4,3,2,1,0:T(8,128)(2,1)}, u32[]{:S(2)}) copy-start(bf16[1,1,1,3,256,256]{5,4,3,2,1,0:T(8,128)(2,1)} %param.6) | copy-start | bytes 1179652
where the time goes:
time: 49.4 us; the launch traced here: 49 us
  waiting for transfers between devices  19.5 us (39%)
  starting transfers between devices  16.3 us (33%)
  local copies, waits for them, and re-layouts  7.96 us (16%)
  matrix products  4.58 us (9%)
    all_to_all x1, waiting for transfers between devices, body(): lax.all_to_all(outgoing, 'gz', split_axis=0, concat_axis=0, tiled=True)  11.5 us
    ppermute x6, starting transfers between devices, shifted(): return lax.ppermute(block, axis, route)  9 us
    ppermute x6, waiting for transfers between devices, shifted(): return lax.ppermute(block, axis, route)  4.44 us
    scatter x1, local copies, waits for them, and re-layouts, body(): outgoing.at[send_slot].set(primal_items)  3.88 us
    all_to_all x1, starting transfers between devices, body(): lax.all_to_all(outgoing, 'gz', split_axis=0, concat_axis=0, tiled=True)  3.86 us
    all_to_all x1, waiting for transfers between devices, body(): lax.all_to_all(answer, 'gz', split_axis=0, concat_axis=0, tiled=True)  3.59 us
    all_to_all x1, starting transfers between devices, body(): lax.all_to_all(answer, 'gz', split_axis=0, concat_axis=0, tiled=True)  3.46 us
    dot_general x1, matrix products, apply_coarse(): lax.dot_general(matrix, stacked, (((0,), (0,)), ((), ())), preferred_elem...  1.77 us
  transfers between devices with their start and end apart: 8, of which 3 were waited for; matrix products, arithmetic and copies ran while one was open for 14% of the time, Pallas kernels for 0%

commit v1 on v0

v1 whole, which is shorter than its diff:
```python
import functools

import jax
import jax.numpy as jnp
from jax import lax
from jax.experimental import pallas as pl
from jax.experimental.pallas import tpu as pltpu
from jax.sharding import PartitionSpec as P

GROUP = 16
BF16 = jnp.bfloat16
F32 = jnp.float32
VMEM = pl.BlockSpec(memory_space=pltpu.VMEM)
SMEM = pl.BlockSpec(memory_space=pltpu.SMEM)


def dot_tn(a, b):
    return lax.dot_general(a, b, (((0,), (0,)), ((), ())), preferred_element_type=F32)


def dot_nn(a, b):
    return lax.dot_general(a, b, (((1,), (0,)), ((), ())), preferred_element_type=F32)


def call(kernel, outs, scratch, args, in_specs=None, flops=0, limit=12 << 20, name=None):
    nbytes = sum(a.size * a.dtype.itemsize for a in args)
    return pl.pallas_call(
        kernel,
        out_shape=outs,
        in_specs=in_specs or [VMEM] * len(args),
        out_specs=jax.tree.map(lambda _: VMEM, outs),
        scratch_shapes=scratch,
        compiler_params=pltpu.CompilerParams(vmem_limit_bytes=limit),
        cost_estimate=pl.CostEstimate(flops=flops, bytes_accessed=nbytes, transcendentals=0),
        name=name,
    )(*args)


def ranks(owner_ref, count_ref, n, items):
    for o in range(n):
        count_ref[o] = 0
    for i in range(items):
        o = owner_ref[i]
        r = count_ref[o]
        count_ref[o] = r + 1
        yield i, o, r


def pack_kernel(n, cap, pf, owner_ref, resid_ref, basis_ref, *refs):
    outs, dual_ref = refs[:n], refs[n]
    slots, count = refs[n + 1], refs[n + 2]
    faces = resid_ref.shape[0]
    per_face = pf // GROUP
    me = lax.axis_index("gz")
    slots[...] = jnp.zeros_like(slots)
    where = {}
    for i, o, r in ranks(owner_ref, count, n, faces * per_face):
        d = lax.rem(o - me + n, n)
        where[i] = d * cap + r
    for k in range(faces):
        t = dot_tn(basis_ref[k], resid_ref[k])
        primal = t[:pf].astype(BF16)
        for g in range(per_face):
            slots[where[k * per_face + g]] = primal[g * GROUP : (g + 1) * GROUP]
        dual = t[pf:].astype(BF16)
        dual_ref[k] = dual
        if k == faces - 1:
            outs[1][cap * GROUP :] = dual
    rows = cap * GROUP
    for d in range(n):
        outs[d][:rows] = slots[d * cap : (d + 1) * cap].reshape(rows, -1)


def coarse_kernel(n, rows, matrix_ref, *refs):
    recv, outs, vec, sol = refs[:n], refs[n : 2 * n], refs[2 * n], refs[2 * n + 1]
    me = lax.axis_index("gz")
    for d in range(n):
        c = lax.rem(me - d + n, n)
        vec[pl.ds(pl.multiple_of(c * rows, GROUP), rows)] = recv[d][:rows]
    sol[...] = dot_tn(matrix_ref[...], vec[...]).astype(BF16)
    for d in range(n):
        c = lax.rem(me + d, n)
        outs[d][...] = sol[pl.ds(pl.multiple_of(c * rows, GROUP), rows)]


def solve_kernel(rows, factor_ref, x_ref, y_ref, z_ref, own_ref, low_ref, high_ref, load):
    df = x_ref.shape[0]
    half = jnp.asarray(0.5, BF16)
    load[:df] = x_ref[...] * half
    load[df : 2 * df] = y_ref[...] * half
    load[2 * df : 3 * df] = z_ref[rows:] * half
    for k in range(3):
        load[(3 + k) * df : (4 + k) * df] = own_ref[k] * half
    h = dot_tn(factor_ref[...], load[...]).astype(BF16)
    s = dot_nn(factor_ref[...], h).astype(BF16)
    for k in range(3):
        low_ref[k] = s[k * df : (k + 1) * df]
        high_ref[k] = s[(3 + k) * df : (4 + k) * df]


def final_kernel(n, cap, pf, owner_ref, basis_ref, x_ref, y_ref, z_ref, high_ref, *refs):
    recv, out_ref, slots, comb, count = refs[:n], refs[n], refs[n + 1], refs[n + 2], refs[n + 3]
    me = lax.axis_index("gz")
    faces = basis_ref.shape[0]
    per_face = pf // GROUP
    for d in range(n):
        slots[d * cap : (d + 1) * cap] = recv[d][...].reshape(cap, GROUP, -1)
    for i, o, r in ranks(owner_ref, count, n, faces * per_face):
        d = lax.rem(me - o + n, n)
        k, g = divmod(i, per_face)
        comb[k, g * GROUP : (g + 1) * GROUP] = slots[d * cap + r]
    for k, above in enumerate((x_ref, y_ref, z_ref)):
        mean = 0.5 * (high_ref[k].astype(F32) + above[...].astype(F32))
        comb[k, pf:] = mean.astype(BF16)
    for k in range(faces):
        out_ref[k] = dot_nn(basis_ref[k], comb[k]).astype(BF16)


def shift(block, axis, distance):
    n = lax.axis_size(axis)
    return lax.ppermute(block, axis, [(i, (i + distance) % n) for i in range(n)])


def body(residual, face_basis, factor, coarse_inv, item_owner):
    resid, basis = residual[0, 0, 0], face_basis[0, 0, 0]
    matrix, inverse = factor[0, 0, 0], coarse_inv[0, 0, 0]
    owners = item_owner[0, 0, 0]
    faces, _, cols = resid.shape
    items = owners.shape[0]
    pf = items * GROUP // faces
    df = resid.shape[1] - pf
    n = lax.axis_size("gz")
    cap = inverse.shape[0] // (n * GROUP)
    rows = cap * GROUP
    flat = lambda r: jax.ShapeDtypeStruct((r, cols), BF16)
    cube = lambda r: jax.ShapeDtypeStruct((faces, r, cols), BF16)

    packed = call(
        functools.partial(pack_kernel, n, cap, pf),
        [flat(rows + df if d == 1 else rows) for d in range(n)] + [cube(df)],
        [pltpu.VMEM((n * cap, GROUP, cols), BF16), pltpu.SMEM((n,), jnp.int32)],
        (owners, resid, basis),
        [SMEM, VMEM, VMEM],
        name="pack",
    )
    sends, dual_own = packed[:n], packed[n]
    recv = [sends[0]] + [shift(sends[d], "gz", d) for d in range(1, n)]
    from_x = shift(dual_own[0], "gx", 1)
    from_y = shift(dual_own[1], "gy", 1)
    low, high = call(
        functools.partial(solve_kernel, rows),
        [cube(df), cube(df)],
        [pltpu.VMEM((matrix.shape[0], cols), BF16)],
        (matrix, from_x, from_y, recv[1], dual_own),
        name="solve",
    )
    back_x = shift(low[0], "gx", -1)
    back_y = shift(low[1], "gy", -1)
    answers = call(
        functools.partial(coarse_kernel, n, rows),
        [flat(rows)] * n,
        [pltpu.VMEM((inverse.shape[0], cols), BF16)] * 2,
        (inverse, *recv),
        name="coarse",
    )
    back = [answers[0]] + [shift(answers[d], "gz", d) for d in range(1, n)]
    back_z = shift(low[2], "gz", -1)
    result = call(
        functools.partial(final_kernel, n, cap, pf),
        cube(pf + df),
        [
            pltpu.VMEM((n * cap, GROUP, cols), BF16),
            pltpu.VMEM((faces, pf + df, cols), BF16),
            pltpu.SMEM((n,), jnp.int32),
        ],
        (owners, basis, back_x, back_y, back_z, high, *back),
        [SMEM] + [VMEM] * (5 + n),
        name="final",
    )
    return result[None, None, None]


def solution(mesh):
    in_specs = (
        P("gx", "gy", "gz", None, None, None),
        P("gx", "gy", "gz", None, None, None),
        P("gx", "gy", "gz", None, None),
        P("gx", "gy", "gz", None, None),
        P("gx", "gy", "gz", None),
    )
    out_specs = P("gx", "gy", "gz", None, None, None)
    return jax.shard_map(body, mesh=mesh, in_specs=in_specs, out_specs=out_specs, check_vma=False)
```

time: 49.4 us -> 33.9 us (0.69)
  waiting for transfers between devices: 19.5 us -> 6.99 us
  matrix products: 4.58 us -> 0 us
  Pallas kernels: 0 us -> 4.5 us
  local copies, waits for them, and re-layouts: 7.96 us -> 3.96 us
  starting transfers between devices: 16.3 us -> 18.1 us
    all_to_all x2 -> x0, waiting for transfers between devices: 15.1 us -> none  [the longest x1 11.5 us: body(): lax.all_to_all(outgoing, 'gz', split_axis=0, concat_axis=0, tiled=True)]
    ppermute x6 -> x11, starting transfers between devices: 9 us -> 18.1 us  [shift(): lax.ppermute(block, axis, [(i, (i + distance) % n) for i in range(n)])]
    all_to_all x2 -> x0, starting transfers between devices: 7.32 us -> none  [the longest x1 3.86 us: body(): lax.all_to_all(outgoing, 'gz', split_axis=0, concat_axis=0, tiled=True)]
    dot_general x4 -> x0, matrix products: 4.58 us -> none  [the longest x1 1.77 us: apply_coarse(): lax.dot_general(matrix, stacked, (((0,), (0,)), ((), ())), preferred_elem...]
    pallas_call x0 -> x4, Pallas kernels: none -> 4.5 us  [call(): pl.pallas_call(kernel, out_shape=outs, in_specs=in_specs or [VMEM] * len(...]
    unnamed x6 -> x14, local copies, waits for them, and re-layouts: 0.01 us -> 3.93 us
    scatter x1 -> x0, local copies, waits for them, and re-layouts: 3.88 us -> none  [body(): outgoing.at[send_slot].set(primal_items)]
    ppermute x6 -> x11, waiting for transfers between devices: 4.44 us -> 6.99 us  [shift(): lax.ppermute(block, axis, [(i, (i + distance) % n) for i in range(n)])]
  transfers between devices with their start and end apart: 8 -> 11, of which waited for: 3 -> 3; matrix products, arithmetic and copies ran while one was open for 14% -> 0% of each run, Pallas kernels for 0% -> 6%
where the time goes in v1:
time: 33.9 us; the launch traced here: 33.6 us
  starting transfers between devices  18.1 us (53%)
  waiting for transfers between devices  6.99 us (21%)
  Pallas kernels  4.5 us (13%)
  local copies, waits for them, and re-layouts  3.96 us (12%)
    ppermute x11, starting transfers between devices, shift(): lax.ppermute(block, axis, [(i, (i + distance) % n) for i in range(n)])  18.1 us
    ppermute x11, waiting for transfers between devices, shift(): lax.ppermute(block, axis, [(i, (i + distance) % n) for i in range(n)])  6.99 us
    pallas_call x4, Pallas kernels, call(): pl.pallas_call(kernel, out_shape=outs, in_specs=in_specs or [VMEM] * len(...  4.5 us
    unnamed x14, local copies, waits for them, and re-layouts  3.93 us
  transfers between devices with their start and end apart: 11, of which 3 were waited for; matrix products, arithmetic and copies ran while one was open for 0% of the time, Pallas kernels for 6%

profile of v1, /device:TPU:0, one launch (start us, length us, event | category | flops | bytes accessed | tf_op | source)
XLA Modules:
  0.0 33.6 jit_solution(8072087557805755181)
XLA Ops:
  0.0 0.0 copy-start
  0.0 1.0 %copy-done = bf16[1,1,1,3,256,256]{5,4,3,2,1,0:T(8,128)(2,1)S(1)} copy-done((bf16[1,1,1,3,256,256]{5,4,3,2,1,0:T(8,128)(2,1)S(1)}, bf16[1,1,1,3,256,256]{5,4,3,2,1,0:T(8,128)(2,1)}, u32[]{:S(2)}) %copy-start) | copy-done | bytes 393240
  1.0 0.0 copy-start.4
  1.0 1.0 %copy-done.4 = bf16[1,1,1,3,256,256]{5,4,3,2,1,0:T(8,128)(2,1)S(1)} copy-done((bf16[1,1,1,3,256,256]{5,4,3,2,1,0:T(8,128)(2,1)S(1)}, bf16[1,1,1,3,256,256]{5,4,3,2,1,0:T(8,128)(2,1)}, u32[]{:S(2)}) %copy-start.4) | copy-done | bytes 393240
  2.0 0.0 copy-start.5
  2.0 0.7 %copy-done.5 = s32[1,1,1,24]{3,2,1,0:T(1,128)S(1)} copy-done((s32[1,1,1,24]{3,2,1,0:T(1,128)S(1)}, s32[1,1,1,24]{3,2,1,0:T(1,128)}, u32[]{:S(2)}) %copy-start.5) | copy-done | bytes 120
  2.6 0.9 %pack.1 = (bf16[192,256]{1,0:T(8,128)(2,1)S(1)}, bf16[320,256]{1,0:T(8,128)(2,1)S(1)}, bf16[192,256]{1,0:T(8,128)(2,1)S(1)}, bf16[192,256]{1,0:T(8,128)(2,1)S(1)}, bf16[3,128,256]{2,1,0:T(8,128)(2,1)S(1)}) custom-call(s32[24]{0:T(128)S(1)} %bitcast.21, bf16[3,256,256]{2,1,0:T(8,128)(2,1)S(1)} %bitcast.20, bf16[3,256,256]{2,1,0:T(8,128)(2,1)S(1)} %bitcast.16), custom_call_target="tpu_custom_call" | custom-call | bytes 786528 | tf_op jit(solution)/shard_map/pack/pallas_call | solution.py:27
  3.5 3.1 %collective-permute-start.2 = (bf16[320,256]{1,0:T(8,128)(2,1)S(1)}, bf16[320,256]{1,0:T(8,128)(2,1)S(1)}, u32[]{:S(2)}, u32[]{:S(2)}) collective-permute-start(bf16[320,256]{1,0:T(8,128)(2,1)S(1)} %get-tuple-element.17), channel_id=1, source_target_pairs={{0,1},{1,2},{2,3},{3,0},{4,5},{5,6},{6,7},{7,4},{8,9},{9,10},{10,1... | collective-permute-start | bytes 491528 | tf_op jit(solution)/shard_map/ppermute | solution.py:121
  6.6 1.6 %collective-permute-start = (bf16[128,256]{1,0:T(8,128)(2,1)S(1)}, bf16[128,256]{1,0:T(8,128)(2,1)S(1)}, u32[]{:S(2)}, u32[]{:S(2)}) collective-permute-start(bf16[128,256]{1,0:T(8,128)(2,1)S(1)} %get-tuple-element.31), channel_id=1, source_target_pairs={{0,16},{16,0},{1,17},{17,1},{2,18},{18,2},{3,19},{19,3},{4,20},{20... | collective-permute-start | bytes 196616 | tf_op jit(solution)/shard_map/ppermute | solution.py:121
  8.2 0.0 collective-permute-start.1
  8.2 2.6 %collective-permute-start.6 = (bf16[192,256]{1,0:T(8,128)(2,1)S(1)}, bf16[192,256]{1,0:T(8,128)(2,1)S(1)}, u32[]{:S(2)}, u32[]{:S(2)}) collective-permute-start(bf16[192,256]{1,0:T(8,128)(2,1)S(1)} %get-tuple-element.21), channel_id=1, source_target_pairs={{0,2},{1,3},{2,0},{3,1},{4,6},{5,7},{6,4},{7,5},{8,10},{9,11},{10,... | collective-permute-start | bytes 294920 | tf_op jit(solution)/shard_map/ppermute | solution.py:121
  10.8 1.3 %collective-permute-start.7 = (bf16[192,256]{1,0:T(8,128)(2,1)S(1)}, bf16[192,256]{1,0:T(8,128)(2,1)S(1)}, u32[]{:S(2)}, u32[]{:S(2)}) collective-permute-start(bf16[192,256]{1,0:T(8,128)(2,1)S(1)} %get-tuple-element.22), channel_id=1, source_target_pairs={{0,3},{1,0},{2,1},{3,2},{4,7},{5,4},{6,5},{7,6},{8,11},{9,8},{10,9... | collective-permute-start | bytes 294920 | tf_op jit(solution)/shard_map/ppermute | solution.py:121
  12.1 0.0 collective-permute-done.x_ref
  12.1 0.0 collective-permute-done.1.y_ref
  12.1 0.7 %collective-permute-done.2.z_ref.refs_1_ = bf16[320,256]{1,0:T(8,128)(2,1)S(1)} collective-permute-done((bf16[320,256]{1,0:T(8,128)(2,1)S(1)}, bf16[320,256]{1,0:T(8,128)(2,1)S(1)}, u32[]{:S(2)}, u32[]{:S(2)}) %collective-permute-start.2) | collective-permute-done | bytes 163872 | tf_op jit(solution)/shard_map/ppermute | solution.py:121
  12.9 0.0 copy-start.2
  12.9 1.3 %copy-done.2 = bf16[1,1,1,768,768]{4,3,2,1,0:T(8,128)(2,1)S(1)} copy-done((bf16[1,1,1,768,768]{4,3,2,1,0:T(8,128)(2,1)S(1)}, bf16[1,1,1,768,768]{4,3,2,1,0:T(8,128)(2,1)}, u32[]{:S(2)}) %copy-start.2) | copy-done | bytes 1179672
  14.1 0.0 copy-start.3
  14.1 1.4 %solve.1 = (bf16[3,128,256]{2,1,0:T(8,128)(2,1)S(1)}, bf16[3,128,256]{2,1,0:T(8,128)(2,1)S(1)}) custom-call(bf16[768,768]{1,0:T(8,128)(2,1)S(1)} %bitcast.18, bf16[128,256]{1,0:T(8,128)(2,1)S(1)} %collective-permute-done.x_ref, bf16[128,256]{1,0:T(8,128)(2,1)S(1)} %collective-permute-done.1.y_ref, bf16[320,256]{1,0:T(8,128)(2,1)S(1)} %collective-permute-done.2.z_ref.refs_1_, ...), custom_call_target="tpu_custom_call" | custom-call | bytes 1671168 | tf_op jit(solution)/shard_map/solve/pallas_call | solution.py:27
  15.5 0.0 copy-start.1
  15.5 0.0 copy-start.6
  15.6 1.6 %collective-permute-start.3 = (bf16[128,256]{1,0:T(8,128)(2,1)S(1)}, bf16[128,256]{1,0:T(8,128)(2,1)S(1)}, u32[]{:S(2)}, u32[]{:S(2)}) collective-permute-start(bf16[128,256]{1,0:T(8,128)(2,1)S(1)} %get-tuple-element.29), channel_id=1, source_target_pairs={{0,16},{16,0},{1,17},{17,1},{2,18},{18,2},{3,19},{19,3},{4,20},{20... | collective-permute-start | bytes 196616 | tf_op jit(solution)/shard_map/ppermute | solution.py:121
  17.2 0.0 collective-permute-done.6.refs_2_
  17.2 0.0 collective-permute-done.7.refs_3_
  17.2 0.0 copy-done.3
  17.2 0.6 %coarse.1 = (bf16[192,256]{1,0:T(8,128)(2,1)S(1)}, bf16[192,256]{1,0:T(8,128)(2,1)S(1)}, bf16[192,256]{1,0:T(8,128)(2,1)S(1)}, bf16[192,256]{1,0:T(8,128)(2,1)S(1)}) custom-call(bf16[768,768]{1,0:T(8,128)(2,1)S(1)} %bitcast.19, bf16[192,256]{1,0:T(8,128)(2,1)S(1)} %get-tuple-element.20.refs_0_, bf16[320,256]{1,0:T(8,128)(2,1)S(1)} %collective-permute-done.2.z_ref.refs_1_, ...), custom_call_target="tpu_custom_call" | custom-call | bytes 1638400 | tf_op jit(solution)/shard_map/coarse/pallas_call | solution.py:27
  17.8 3.4 %collective-permute-start.10 = (bf16[192,256]{1,0:T(8,128)(2,1)S(1)}, bf16[192,256]{1,0:T(8,128)(2,1)S(1)}, u32[]{:S(2)}, u32[]{:S(2)}) collective-permute-start(bf16[192,256]{1,0:T(8,128)(2,1)S(1)} %get-tuple-element.26), channel_id=1, source_target_pairs={{0,3},{1,0},{2,1},{3,2},{4,7},{5,4},{6,5},{7,6},{8,11},{9,8},{10,9... | collective-permute-start | bytes 294920 | tf_op jit(solution)/shard_map/ppermute | solution.py:121
  21.2 0.0 collective-permute-start.8
  21.2 0.6 %collective-permute-start.9 = (bf16[192,256]{1,0:T(8,128)(2,1)S(1)}, bf16[192,256]{1,0:T(8,128)(2,1)S(1)}, u32[]{:S(2)}, u32[]{:S(2)}) collective-permute-start(bf16[192,256]{1,0:T(8,128)(2,1)S(1)} %get-tuple-element.25), channel_id=1, source_target_pairs={{0,2},{1,3},{2,0},{3,1},{4,6},{5,7},{6,4},{7,5},{8,10},{9,11},{10,... | collective-permute-start | bytes 294920 | tf_op jit(solution)/shard_map/ppermute | solution.py:121
  21.9 0.7 %collective-permute-start.4 = (bf16[128,256]{1,0:T(8,128)(2,1)S(1)}, bf16[128,256]{1,0:T(8,128)(2,1)S(1)}, u32[]{:S(2)}, u32[]{:S(2)}) collective-permute-start(bf16[128,256]{1,0:T(8,128)(2,1)S(1)} %get-tuple-element.28), channel_id=1, source_target_pairs={{0,12},{4,0},{8,4},{12,8},{1,13},{5,1},{9,5},{13,9},{2,14},{6,2},{... | collective-permute-start | bytes 196616 | tf_op jit(solution)/shard_map/ppermute | solution.py:121
  22.6 0.0 collective-permute-done.3.x_ref
  22.6 3.1 %collective-permute-start.5 = (bf16[128,256]{1,0:T(8,128)(2,1)S(1)}, bf16[128,256]{1,0:T(8,128)(2,1)S(1)}, u32[]{:S(2)}, u32[]{:S(2)}) collective-permute-start(bf16[128,256]{1,0:T(8,128)(2,1)S(1)} %get-tuple-element.27), channel_id=1, source_target_pairs={{0,3},{1,0},{2,1},{3,2},{4,7},{5,4},{6,5},{7,6},{8,11},{9,8},{10,9... | collective-permute-start | bytes 196616 | tf_op jit(solution)/shard_map/ppermute | solution.py:121
  25.7 0.0 collective-permute-done.4.y_ref
  25.7 3.9 %collective-permute-done.5.z_ref = bf16[128,256]{1,0:T(8,128)(2,1)S(1)} collective-permute-done((bf16[128,256]{1,0:T(8,128)(2,1)S(1)}, bf16[128,256]{1,0:T(8,128)(2,1)S(1)}, u32[]{:S(2)}, u32[]{:S(2)}) %collective-permute-start.5) | collective-permute-done | bytes 65568 | tf_op jit(solution)/shard_map/ppermute | solution.py:121
  29.7 0.0 collective-permute-done.10.refs_3_
  29.7 0.0 collective-permute-done.8.refs_1_
  29.7 2.3 %collective-permute-done.9.refs_2_ = bf16[192,256]{1,0:T(8,128)(2,1)S(1)} collective-permute-done((bf16[192,256]{1,0:T(8,128)(2,1)S(1)}, bf16[192,256]{1,0:T(8,128)(2,1)S(1)}, u32[]{:S(2)}, u32[]{:S(2)}) %collective-permute-start.9) | collective-permute-done | bytes 98336 | tf_op jit(solution)/shard_map/ppermute | solution.py:121
  32.0 0.0 copy-done.1
  32.0 0.0 copy-done.6
  32.0 1.6 %final.1 = bf16[3,256,256]{2,1,0:T(8,128)(2,1)} custom-call(s32[24]{0:T(128)S(1)} %bitcast.22, bf16[3,256,256]{2,1,0:T(8,128)(2,1)S(1)} %bitcast.17, bf16[128,256]{1,0:T(8,128)(2,1)S(1)} %collective-permute-done.3.x_ref, bf16[128,256]{1,0:T(8,128)(2,1)S(1)} %collective-permute-done.4.y_ref, bf16[128,256]{1,0:T(8,128)(2,1)S(1)} %collective-permute-done.5.z_ref, ...), custom_call_target="tpu_custom_call" | custom-call | bytes 1179744 | tf_op jit(solution)/shard_map/final/pallas_call | solution.py:27
  (2 shorter events, 0.0 us)
Async XLA Ops:
  0.0 1.0 %copy-start = (bf16[1,1,1,3,256,256]{5,4,3,2,1,0:T(8,128)(2,1)S(1)}, bf16[1,1,1,3,256,256]{5,4,3,2,1,0:T(8,128)(2,1)}, u32[]{:S(2)}) copy-start(bf16[1,1,1,3,256,256]{5,4,3,2,1,0:T(8,128)(2,1)} %param.6) | copy-start | bytes 1179652
  1.0 1.0 %copy-start.4 = (bf16[1,1,1,3,256,256]{5,4,3,2,1,0:T(8,128)(2,1)S(1)}, bf16[1,1,1,3,256,256]{5,4,3,2,1,0:T(8,128)(2,1)}, u32[]{:S(2)}) copy-start(bf16[1,1,1,3,256,256]{5,4,3,2,1,0:T(8,128)(2,1)} %param.5) | copy-start | bytes 1179652
  2.0 0.7 %copy-start.5 = (s32[1,1,1,24]{3,2,1,0:T(1,128)S(1)}, s32[1,1,1,24]{3,2,1,0:T(1,128)}, u32[]{:S(2)}) copy-start(s32[1,1,1,24]{3,2,1,0:T(1,128)} %param.9) | copy-start | bytes 292
  3.5 9.3 %collective-permute-start.2 = (bf16[320,256]{1,0:T(8,128)(2,1)S(1)}, bf16[320,256]{1,0:T(8,128)(2,1)S(1)}, u32[]{:S(2)}, u32[]{:S(2)}) collective-permute-start(bf16[320,256]{1,0:T(8,128)(2,1)S(1)} %get-tuple-element.17), channel_id=1, source_target_pairs={{0,1},{1,2},{2,3},{3,0},{4,5},{5,6},{6,7},{7,4},{8,9},{9,10},{10,1... | collective-permute-start | bytes 491528 | tf_op jit(solution)/shard_map/ppermute | solution.py:121
  6.6 5.5 %collective-permute-start = (bf16[128,256]{1,0:T(8,128)(2,1)S(1)}, bf16[128,256]{1,0:T(8,128)(2,1)S(1)}, u32[]{:S(2)}, u32[]{:S(2)}) collective-permute-start(bf16[128,256]{1,0:T(8,128)(2,1)S(1)} %get-tuple-element.31), channel_id=1, source_target_pairs={{0,16},{16,0},{1,17},{17,1},{2,18},{18,2},{3,19},{19,3},{4,20},{20... | collective-permute-start | bytes 196616 | tf_op jit(solution)/shard_map/ppermute | solution.py:121
  8.2 3.9 %collective-permute-start.1 = (bf16[128,256]{1,0:T(8,128)(2,1)S(1)}, bf16[128,256]{1,0:T(8,128)(2,1)S(1)}, u32[]{:S(2)}, u32[]{:S(2)}) collective-permute-start(bf16[128,256]{1,0:T(8,128)(2,1)S(1)} %get-tuple-element.30), channel_id=1, source_target_pairs={{0,4},{4,8},{8,12},{12,0},{1,5},{5,9},{9,13},{13,1},{2,6},{6,10},{... | collective-permute-start | bytes 196616 | tf_op jit(solution)/shard_map/ppermute | solution.py:121
  8.2 9.0 %collective-permute-start.6 = (bf16[192,256]{1,0:T(8,128)(2,1)S(1)}, bf16[192,256]{1,0:T(8,128)(2,1)S(1)}, u32[]{:S(2)}, u32[]{:S(2)}) collective-permute-start(bf16[192,256]{1,0:T(8,128)(2,1)S(1)} %get-tuple-element.21), channel_id=1, source_target_pairs={{0,2},{1,3},{2,0},{3,1},{4,6},{5,7},{6,4},{7,5},{8,10},{9,11},{10,... | collective-permute-start | bytes 294920 | tf_op jit(solution)/shard_map/ppermute | solution.py:121
  10.8 6.4 %collective-permute-start.7 = (bf16[192,256]{1,0:T(8,128)(2,1)S(1)}, bf16[192,256]{1,0:T(8,128)(2,1)S(1)}, u32[]{:S(2)}, u32[]{:S(2)}) collective-permute-start(bf16[192,256]{1,0:T(8,128)(2,1)S(1)} %get-tuple-element.22), channel_id=1, source_target_pairs={{0,3},{1,0},{2,1},{3,2},{4,7},{5,4},{6,5},{7,6},{8,11},{9,8},{10,9... | collective-permute-start | bytes 294920 | tf_op jit(solution)/shard_map/ppermute | solution.py:121
  12.9 1.3 %copy-start.2 = (bf16[1,1,1,768,768]{4,3,2,1,0:T(8,128)(2,1)S(1)}, bf16[1,1,1,768,768]{4,3,2,1,0:T(8,128)(2,1)}, u32[]{:S(2)}) copy-start(bf16[1,1,1,768,768]{4,3,2,1,0:T(8,128)(2,1)} %param.7) | copy-start | bytes 3538948
  14.1 3.1 %copy-start.3 = (bf16[1,1,1,768,768]{4,3,2,1,0:T(8,128)(2,1)S(1)}, bf16[1,1,1,768,768]{4,3,2,1,0:T(8,128)(2,1)}, u32[]{:S(2)}) copy-start(bf16[1,1,1,768,768]{4,3,2,1,0:T(8,128)(2,1)} %param.8) | copy-start | bytes 3538948
  15.5 16.5 %copy-start.1 = (bf16[1,1,1,3,256,256]{5,4,3,2,1,0:T(8,128)(2,1)S(1)}, bf16[1,1,1,3,256,256]{5,4,3,2,1,0:T(8,128)(2,1)}, u32[]{:S(2)}) copy-start(bf16[1,1,1,3,256,256]{5,4,3,2,1,0:T(8,128)(2,1)} %param.6) | copy-start | bytes 1179652
  15.5 16.5 %copy-start.6 = (s32[1,1,1,24]{3,2,1,0:T(1,128)S(1)}, s32[1,1,1,24]{3,2,1,0:T(1,128)}, u32[]{:S(2)}) copy-start(s32[1,1,1,24]{3,2,1,0:T(1,128)} %param.9) | copy-start | bytes 292
  15.6 7.0 %collective-permute-start.3 = (bf16[128,256]{1,0:T(8,128)(2,1)S(1)}, bf16[128,256]{1,0:T(8,128)(2,1)S(1)}, u32[]{:S(2)}, u32[]{:S(2)}) collective-permute-start(bf16[128,256]{1,0:T(8,128)(2,1)S(1)} %get-tuple-element.29), channel_id=1, source_target_pairs={{0,16},{16,0},{1,17},{17,1},{2,18},{18,2},{3,19},{19,3},{4,20},{20... | collective-permute-start | bytes 196616 | tf_op jit(solution)/shard_map/ppermute | solution.py:121
  17.8 11.8 %collective-permute-start.10 = (bf16[192,256]{1,0:T(8,128)(2,1)S(1)}, bf16[192,256]{1,0:T(8,128)(2,1)S(1)}, u32[]{:S(2)}, u32[]{:S(2)}) collective-permute-start(bf16[192,256]{1,0:T(8,128)(2,1)S(1)} %get-tuple-element.26), channel_id=1, source_target_pairs={{0,3},{1,0},{2,1},{3,2},{4,7},{5,4},{6,5},{7,6},{8,11},{9,8},{10,9... | collective-permute-start | bytes 294920 | tf_op jit(solution)/shard_map/ppermute | solution.py:121
  21.2 8.4 %collective-permute-start.8 = (bf16[192,256]{1,0:T(8,128)(2,1)S(1)}, bf16[192,256]{1,0:T(8,128)(2,1)S(1)}, u32[]{:S(2)}, u32[]{:S(2)}) collective-permute-start(bf16[192,256]{1,0:T(8,128)(2,1)S(1)} %get-tuple-element.24), channel_id=1, source_target_pairs={{0,1},{1,2},{2,3},{3,0},{4,5},{5,6},{6,7},{7,4},{8,9},{9,10},{10,1... | collective-permute-start | bytes 294920 | tf_op jit(solution)/shard_map/ppermute | solution.py:121
  21.2 10.7 %collective-permute-start.9 = (bf16[192,256]{1,0:T(8,128)(2,1)S(1)}, bf16[192,256]{1,0:T(8,128)(2,1)S(1)}, u32[]{:S(2)}, u32[]{:S(2)}) collective-permute-start(bf16[192,256]{1,0:T(8,128)(2,1)S(1)} %get-tuple-element.25), channel_id=1, source_target_pairs={{0,2},{1,3},{2,0},{3,1},{4,6},{5,7},{6,4},{7,5},{8,10},{9,11},{10,... | collective-permute-start | bytes 294920 | tf_op jit(solution)/shard_map/ppermute | solution.py:121
  21.9 3.8 %collective-permute-start.4 = (bf16[128,256]{1,0:T(8,128)(2,1)S(1)}, bf16[128,256]{1,0:T(8,128)(2,1)S(1)}, u32[]{:S(2)}, u32[]{:S(2)}) collective-permute-start(bf16[128,256]{1,0:T(8,128)(2,1)S(1)} %get-tuple-element.28), channel_id=1, source_target_pairs={{0,12},{4,0},{8,4},{12,8},{1,13},{5,1},{9,5},{13,9},{2,14},{6,2},{... | collective-permute-start | bytes 196616 | tf_op jit(solution)/shard_map/ppermute | solution.py:121
  22.6 7.1 %collective-permute-start.5 = (bf16[128,256]{1,0:T(8,128)(2,1)S(1)}, bf16[128,256]{1,0:T(8,128)(2,1)S(1)}, u32[]{:S(2)}, u32[]{:S(2)}) collective-permute-start(bf16[128,256]{1,0:T(8,128)(2,1)S(1)} %get-tuple-element.27), channel_id=1, source_target_pairs={{0,3},{1,0},{2,1},{3,2},{4,7},{5,4},{6,5},{7,6},{8,11},{9,8},{10,9... | collective-permute-start | bytes 196616 | tf_op jit(solution)/shard_map/ppermute | solution.py:121
